TPU v7x, 128 devices: a whole 4x4x4 slice. The times are simulated.
128 devices in a mesh: seq: 32 (over x_lo, y, z), head: 4 (over x_hi, core).
Axes of the slice: x: 4 (x_hi: 2, x_lo: 2; x = x_hi * 2 + x_lo), y: 4, z: 4, core: 2. Of those that a mesh axis runs over, the one named last changes fastest.
Arguments:
- tokens: bfloat16 [32768, 2048], P('seq'), may hold values from -26 to 26, as said below
- w_query: bfloat16 [2048, 2048], P(None, 'head'), as said below
- w_key: bfloat16 [2048, 2048], P(None, 'head'), as said below
- w_value: bfloat16 [2048, 2048], P(None, 'head'), may hold values from -0.125 to 0.125
- w_out: bfloat16 [2048, 2048], P('head'), may hold values from -0.125 to 0.125
- window_blocks: int32 [256, 3], P('seq'), may hold values from 0 to 255, as said below
- random_blocks: int32 [256, 4], replicated, may hold values from 0 to 255, as said below
- summary_blocks: int32 [256, 2], P('seq'), may hold values from 0 to 3
- seg_start: int32 [512], replicated, may hold values from 0 to 32767, as said below
- seg_end: int32 [512], replicated, may hold values from 1 to 32768, as said below
Outputs:
- mixed: bfloat16 [32768, 2048], P('seq', 'head')
Inputs may be any that keep to these rules, and one draw needn't show every extreme that they name: `tokens`: finite activations. `w_query`: a projection scaled by its fan-in. `w_key`: a projection scaled by its fan-in. `window_blocks`: row i names block i first, then two other blocks at most 2 blocks away from i. `random_blocks`: in the rows of one index of seq (aligned runs of 8 rows), the blocks held by any one index of seq are named at most 2 times, and those of some index exactly 2 times. `seg_start`: each segment holds 1 to 512 tokens, segment 0 exactly 512; segment s lies within the tokens of one index of seq, namely index (s // 16 + 16) mod 32. seg_end is greater than seg_start and at most seg_start + 512.
All inputs are finite; a program needn't handle non-finite values.
Results may differ from a plain program's by a relative error of at most 0.0095.
Values may be sent and summed in bfloat16 or wider, within the bound.
A program may use at most 192 MiB of HBM per device.

v0:
```python
import jax
import jax.numpy as jnp
from jax import lax
from jax.sharding import PartitionSpec as P

HD = 128
BLK = 128
WIN = 3
R = 4
FIXL = 2


def cut_along(array, dim, count):
    before, after = (array.shape[:dim], array.shape[dim + 1 :])
    return jnp.moveaxis(array.reshape(*before, count, -1, *after), dim, 0)


def summed_on_arrival(array, axis, dim):
    count = lax.axis_size(axis)
    parts = lax.all_to_all(cut_along(array, dim, count), axis, 0, 0, tiled=True)
    return jnp.sum(parts, axis=0)


def in_order(parts, dim):
    parts = jnp.moveaxis(parts, 0, dim)
    lengths = parts.shape
    return parts.reshape(*lengths[:dim], lengths[dim] * lengths[dim + 1], *lengths[dim + 2 :])


def sent_to_all(array, axis):
    count = lax.axis_size(axis)
    return lax.all_to_all(
        jnp.broadcast_to(array[None], (count, *array.shape)), axis, 0, 0, tiled=True
    )


def gather_directly(array, axis, dim):
    return in_order(sent_to_all(array, axis), dim)


def with_halo(block, sides, width):
    for axis, dim in sides:
        count = lax.axis_size(axis)
        forward = [(i, i + 1) for i in range(count - 1)]
        backward = [(target, source) for source, target in forward]
        low = lax.ppermute(
            lax.slice_in_dim(block, block.shape[dim] - width, None, axis=dim), axis, forward
        )
        high = lax.ppermute(lax.slice_in_dim(block, 0, width, axis=dim), axis, backward)
        block = jnp.concatenate([low, block, high], axis=dim)
    return block


def sent_and_summed(array, axis, dim):
    parts = cut_along(array, dim, lax.axis_size(axis))
    arrived = lax.all_to_all(parts, axis, split_axis=0, concat_axis=0, tiled=True)
    return arrived.astype(jnp.float32).sum(axis=0)


def project(tokens, weight):
    return jnp.dot(tokens, weight, preferred_element_type=jnp.float32).astype(jnp.bfloat16)


def rank_refs(random_blocks, devices, block_count):
    ref_lists = random_blocks.reshape(devices, -1)
    owners = ref_lists // block_count
    within = ref_lists - owners * block_count
    ref_count = ref_lists.shape[1]
    same_owner = (owners[:, :, None] == owners[:, None, :]).astype(jnp.int32)
    earlier = (
        lax.iota(jnp.int32, ref_count)[None, :] < lax.iota(jnp.int32, ref_count)[:, None]
    ).astype(jnp.int32)
    ranking = jnp.sum(same_owner * earlier[None, :, :], axis=2)
    return (owners, within, ranking)


def per_device(
    tokens,
    w_query,
    w_key,
    w_value,
    w_out,
    window_blocks,
    random_blocks,
    summary_blocks,
    seg_start,
    seg_end,
):
    tok_rows = tokens.shape[0]
    columns = w_query.shape[1]
    head_count = columns // HD
    block_count = tok_rows // BLK
    devices = lax.axis_size("seq")
    my_index = lax.axis_index("seq")
    ref_count = block_count * R
    slot_count = max(2, (3 * ref_count + 2 * devices - 1) // (2 * devices))
    queries = project(tokens, w_query)
    key_rows = project(tokens, w_key)
    values = project(tokens, w_value)
    key_value = jnp.stack([key_rows, values], axis=1)
    blocks = key_value.reshape(block_count, BLK, 2, columns)
    position = my_index * tok_rows + lax.iota(jnp.int32, tok_rows)
    member = (
        (position[None, :] >= seg_start[:, None]) & (position[None, :] < seg_end[:, None])
    ).astype(jnp.bfloat16)
    partial_sums = jnp.dot(
        member, key_value.reshape(tok_rows, 2 * columns), preferred_element_type=jnp.float32
    )
    counts = (seg_end - seg_start).astype(jnp.float32)
    share_rows = summed_on_arrival(partial_sums, "seq", 0)
    share_count = share_rows.shape[0]
    own_counts = lax.dynamic_slice_in_dim(counts, my_index * share_count, share_count)
    local_means = (share_rows / own_counts[:, None]).astype(jnp.bfloat16)
    means = gather_directly(local_means, "seq", 0)
    summary = means.reshape(-1, BLK, 2, columns)
    owners, within, ranking = rank_refs(random_blocks, devices, block_count)
    slot_ids = lax.iota(jnp.int32, slot_count)
    chosen = (
        (owners == my_index)[:, :, None] & (ranking[:, :, None] == slot_ids[None, None, :])
    ).astype(jnp.int32)
    send_index = jnp.sum(chosen * within[:, :, None], axis=1)
    outgoing = blocks[send_index]
    mine_owner = lax.dynamic_index_in_dim(owners, my_index, 0, keepdims=False)
    mine_rank = lax.dynamic_index_in_dim(ranking, my_index, 0, keepdims=False)
    arrived = lax.all_to_all(outgoing, "seq", split_axis=0, concat_axis=0, tiled=True)
    padded = with_halo(key_value, (("seq", 0),), 2 * BLK)
    nearby = padded.reshape(block_count + 4, BLK, 2, columns)
    fetched = arrived.reshape(devices * slot_count, BLK, 2, columns)
    random_index = (mine_owner * slot_count + mine_rank).reshape(block_count, R)
    window_index = window_blocks - my_index * block_count + 2
    group_size = min(4, block_count)
    group_count = block_count // group_size
    score_scale = HD ** (-0.5)

    def attend(inputs):
        block_queries, window_ids, random_ids, summary_ids = inputs
        gathered = jnp.concatenate(
            [nearby[window_ids], fetched[random_ids], summary[summary_ids]], axis=1
        )
        key_count = gathered.shape[1] * BLK
        gathered = gathered.reshape(group_size, key_count, 2, head_count, HD)
        scores = (
            jnp.einsum(
                "gqhd,gkhd->ghqk",
                block_queries,
                gathered[:, :, 0],
                preferred_element_type=jnp.float32,
            )
            * score_scale
        )
        row_peak = jnp.max(scores, axis=-1, keepdims=True)
        weights = jnp.exp(scores - row_peak)
        row_total = jnp.sum(weights, axis=-1)
        mixed = jnp.einsum(
            "ghqk,gkhd->gqhd",
            weights.astype(jnp.bfloat16),
            gathered[:, :, 1],
            preferred_element_type=jnp.float32,
        )
        mixed = mixed / jnp.transpose(row_total, (0, 2, 1))[..., None]
        return mixed.astype(jnp.bfloat16)

    attended = lax.map(
        attend,
        (
            queries.reshape(group_count, group_size, BLK, head_count, HD),
            window_index.reshape(group_count, group_size, WIN),
            random_index.reshape(group_count, group_size, R),
            summary_blocks.reshape(group_count, group_size, FIXL),
        ),
    )
    attended = attended.reshape(tok_rows, columns)
    partial_value = jnp.dot(attended, w_out, preferred_element_type=jnp.float32)
    return sent_and_summed(partial_value.astype(jnp.bfloat16), "head", 1).astype(jnp.bfloat16)


def solution(mesh):
    placed = (
        P("seq", None),
        P(None, "head"),
        P(None, "head"),
        P(None, "head"),
        P("head", None),
        P("seq", None),
        P(),
        P("seq", None),
        P(),
        P(),
    )
    return jax.shard_map(
        per_device, mesh=mesh, in_specs=placed, out_specs=P("seq", "head"), check_vma=False
    )
```

profile of v0, /device:TPU:120, one launch (start us, length us, event | category | flops | bytes accessed | tf_op | source)
XLA Modules:
  0.0 657.2 jit_solution(5133711333637323551)
XLA Ops:
  18.5 8.0 %all-to-all-start.1 = ((f32[32,16,1024]{2,1,0:T(8,128)}), f32[32,16,1024]{2,1,0:T(8,128)}, u32[]{:S(2)}, u32[]{:S(2)}) async-start(f32[32,16,1024]{2,1,0:T(8,128)} %fusion.23), calls=%async_computation.1 | async-start | bytes 4194304 | tf_op jit(solution)/shard_map/all_to_all | solution.py:20
  26.9 24.8 %all-to-all-done.1 = f32[32,16,1024]{2,1,0:T(8,128)} async-done(((f32[32,16,1024]{2,1,0:T(8,128)}), f32[32,16,1024]{2,1,0:T(8,128)}, u32[]{:S(2)}, u32[]{:S(2)}) %all-to-all-start.1) | async-done | bytes 2097184 | tf_op jit(solution)/shard_map/all_to_all | solution.py:20
  54.5 8.1 %all-to-all-start.2 = ((bf16[32,16,1024]{2,1,0:T(8,128)(2,1)}), bf16[32,16,1024]{2,1,0:T(8,128)(2,1)}, u32[]{:S(2)}, u32[]{:S(2)}) async-start(bf16[32,16,1024]{2,1,0:T(8,128)(2,1)} %broadcast_in_dim.8), calls=%async_computation.2 | async-start | bytes 2097152 | tf_op jit(solution)/shard_map/all_to_all | solution.py:32
  66.6 9.0 %gather_fusion.3 = bf16[64,128,2,512]{3,1,2,0:T(8,128)(2,1)} fusion(bf16[8,128,2,512]{3,1,0,2:T(8,128)(2,1)} %pad_maximum_fusion.3, s32[1024]{0:T(1024)S(1)} %pad_clamp_fusion.3), kind=kCustom, calls=%fused_computation.3 | custom fusion | bytes 33554688 | tf_op jit(solution)/shard_map/gather | solution.py:122
  75.6 30.7 %copy.61 = bf16[32,2,128,2,512]{4,3,2,1,0:T(2,128)(2,1)} copy(bf16[32,2,128,2,512]{4,2,3,1,0:T(8,128)(2,1)} %bitcast.113) | data formatting | bytes 33554432 | tf_op jit(solution)/shard_map/gather | solution.py:122
  106.3 8.5 %all-to-all-start = ((bf16[32,2,128,2,512]{4,3,2,1,0:T(2,128)(2,1)}), bf16[32,2,128,2,512]{4,3,2,1,0:T(2,128)(2,1)}, u32[]{:S(2)}, u32[]{:S(2)}) async-start(bf16[32,2,128,2,512]{4,3,2,1,0:T(2,128)(2,1)} %copy.61), calls=%async_computation | async-start | bytes 33554432 | tf_op jit(solution)/shard_map/all_to_all | solution.py:125
  131.5 237.6 %collective-permute-done = bf16[256,2,512]{2,0,1:T(8,128)(2,1)} collective-permute-done((bf16[256,2,512]{2,0,1:T(8,128)(2,1)}, bf16[256,2,512]{2,0,1:T(8,128)(2,1)}, u32[]{:S(2)}, u32[]{:S(2)}) %collective-permute-start) | collective-permute-done | bytes 524320 | tf_op jit(solution)/shard_map/ppermute | solution.py:46
  369.1 20.4 %collective-permute-done.1 = bf16[256,2,512]{2,0,1:T(8,128)(2,1)} collective-permute-done((bf16[256,2,512]{2,0,1:T(8,128)(2,1)}, bf16[256,2,512]{2,0,1:T(8,128)(2,1)}, u32[]{:S(2)}, u32[]{:S(2)}) %collective-permute-start.1) | collective-permute-done | bytes 524320 | tf_op jit(solution)/shard_map/ppermute | solution.py:49
  397.9 197.4 %while.10 = (s32[]{:T(128)}, bf16[2,4,128,4,128]{4,3,2,1,0:T(4,128)(2,1)}, s32[2,4,3]{1,0,2:T(2,128)S(1)}, bf16[12,128,2,512]{3,2,1,0:T(2,128)(2,1)}, s32[2,4,4]...) while((s32[]{:T(128)}, ...), condition=%wide.region_6.7_spmd, body=%wide.region_3.6_spmd.sunk | while | flops 1236794496 | bytes 204527360 | solution.py:163
  398.1 15.7 %gather_fusion.1 = bf16[16,128,2,512]{3,2,1,0:T(2,128)(2,1)} fusion(bf16[64,128,2,512]{3,2,1,0:T(2,128)(2,1)} %get-tuple-element.203, s32[1024]{0:T(1024)S(1)} %pad_clamp_fusion.8), kind=kCustom, calls=%fused_computation.1.clone.1 | custom fusion | bytes 8388672 | tf_op jit(solution)/shard_map/while/body/eval_jaxpr/gather | solution.py:138
  419.1 9.8 %gather_fusion.2 = bf16[12,128,2,512]{3,2,1,0:T(2,128)(2,1)} fusion(bf16[12,128,2,512]{3,2,1,0:T(2,128)(2,1)} %get-tuple-element.201, s32[1024]{0:T(1024)S(1)} %pad_clamp_fusion.9), kind=kCustom, calls=%fused_computation.clone.1 | custom fusion | bytes 6291504 | tf_op jit(solution)/shard_map/while/body/eval_jaxpr/gather | solution.py:138
  441.8 6.3 pad_maximum_fusion.5
  448.1 13.9 %reshape.354 = bf16[4,1152,2,4,128]{4,3,1,2,0:T(4,128)(2,1)} reshape(bf16[4,9,128,2,512]{4,2,1,3,0:T(8,128)(2,1)} %pad_maximum_fusion.5) | data formatting | bytes 18874368 | tf_op jit(solution)/shard_map/while/body/eval_jaxpr/reshape | solution.py:141
  462.0 8.8 %fusion.54 = (bf16[4,1152,1,4,128]{4,3,1,2,0:T(4,128)(2,1)}, bf16[4,1152,1,4,128]{4,3,1,2,0:T(4,128)(2,1)S(1)}) fusion(bf16[4,1152,2,4,128]{4,3,1,2,0:T(4,128)(2,1)} %reshape.354), kind=kLoop, calls=%fused_computation.74.clone.1 | loop fusion | bytes 18874368 | tf_op jit(solution)/shard_map/while/body/eval_jaxpr/slice | solution.py:157
  476.4 8.2 %copy.110 = bf16[4,1152,1,4,128]{1,4,3,0,2:T(8,128)(2,1)} copy(bf16[4,1152,1,4,128]{4,3,1,2,0:T(4,128)(2,1)} %get-tuple-element.177) | data formatting | bytes 9437184 | tf_op jit(solution)/shard_map/while
  484.6 7.9 %fusion.56 = bf16[1,4,128,4,128]{2,4,3,1,0:T(8,128)(2,1)} fusion(f32[4,4,128,1152]{3,2,1,0:T(8,128)} %copy-done.1, f32[4,4,128]{2,1,0:T(4,128)S(1)} %get-tuple-element.176, bf16[4,1152,1,4,128]{1,4,3,0,2:T(8,128)(2,1)} %copy.110, f32[4,128,4]{1,2,0:T(4,128)S(1)} %bitcast.126), kind=kOutput, calls=%fused_computation.17.clone.1 | convolution fusion | flops 611581952 | bytes 14696448 | tf_op jit(solution)/shard_map/while/body/eval_jaxpr/ghqk,gkhd->gqhd/dot_general | solution.py:154
  496.8 15.7 %gather_fusion.1 = bf16[16,128,2,512]{3,2,1,0:T(2,128)(2,1)} fusion(bf16[64,128,2,512]{3,2,1,0:T(2,128)(2,1)} %get-tuple-element.203, s32[1024]{0:T(1024)S(1)} %pad_clamp_fusion.8), kind=kCustom, calls=%fused_computation.1.clone.1 | custom fusion | bytes 8388672 | tf_op jit(solution)/shard_map/while/body/eval_jaxpr/gather | solution.py:138
  517.7 9.7 %gather_fusion.2 = bf16[12,128,2,512]{3,2,1,0:T(2,128)(2,1)} fusion(bf16[12,128,2,512]{3,2,1,0:T(2,128)(2,1)} %get-tuple-element.201, s32[1024]{0:T(1024)S(1)} %pad_clamp_fusion.9), kind=kCustom, calls=%fused_computation.clone.1 | custom fusion | bytes 6291504 | tf_op jit(solution)/shard_map/while/body/eval_jaxpr/gather | solution.py:138
  540.4 6.3 pad_maximum_fusion.5
  546.7 13.9 %reshape.354 = bf16[4,1152,2,4,128]{4,3,1,2,0:T(4,128)(2,1)} reshape(bf16[4,9,128,2,512]{4,2,1,3,0:T(8,128)(2,1)} %pad_maximum_fusion.5) | data formatting | bytes 18874368 | tf_op jit(solution)/shard_map/while/body/eval_jaxpr/reshape | solution.py:141
  560.7 8.8 %fusion.54 = (bf16[4,1152,1,4,128]{4,3,1,2,0:T(4,128)(2,1)}, bf16[4,1152,1,4,128]{4,3,1,2,0:T(4,128)(2,1)S(1)}) fusion(bf16[4,1152,2,4,128]{4,3,1,2,0:T(4,128)(2,1)} %reshape.354), kind=kLoop, calls=%fused_computation.74.clone.1 | loop fusion | bytes 18874368 | tf_op jit(solution)/shard_map/while/body/eval_jaxpr/slice | solution.py:157
  575.0 8.2 %copy.110 = bf16[4,1152,1,4,128]{1,4,3,0,2:T(8,128)(2,1)} copy(bf16[4,1152,1,4,128]{4,3,1,2,0:T(4,128)(2,1)} %get-tuple-element.177) | data formatting | bytes 9437184 | tf_op jit(solution)/shard_map/while
  583.3 7.9 %fusion.56 = bf16[1,4,128,4,128]{2,4,3,1,0:T(8,128)(2,1)} fusion(f32[4,4,128,1152]{3,2,1,0:T(8,128)} %copy-done.1, f32[4,4,128]{2,1,0:T(4,128)S(1)} %get-tuple-element.176, bf16[4,1152,1,4,128]{1,4,3,0,2:T(8,128)(2,1)} %copy.110, f32[4,128,4]{1,2,0:T(4,128)S(1)} %bitcast.126), kind=kOutput, calls=%fused_computation.17.clone.1 | convolution fusion | flops 611581952 | bytes 14696448 | tf_op jit(solution)/shard_map/while/body/eval_jaxpr/ghqk,gkhd->gqhd/dot_general | solution.py:154
  599.3 53.7 %all_to_all.20 = bf16[4,1024,512]{2,1,0:T(8,128)(2,1)} all-to-all(bf16[4,1024,512]{2,1,0:T(8,128)(2,1)S(1)} %bitcast.114), channel_id=1, replica_groups=mesh['seq'=32,'head'=4] {'head'}, dimensions={0} | all-to-all | bytes 8388608 | tf_op jit(solution)/shard_map/all_to_all | solution.py:56
  (116 shorter events, 114.6 us)
Async XLA Ops:
  0.0 595.3 %copy-start = (bf16[512,2048]{1,0:T(8,128)(2,1)S(1)}, bf16[512,2048]{1,0:T(8,128)(2,1)}, u32[]{:S(2)}) copy-start(bf16[512,2048]{1,0:T(8,128)(2,1)} %param.16) | copy-start | bytes 6291460
  0.0 5.3 copy-start.10
  0.0 5.3 copy-start.11
  7.7 1.0 copy-start.3
  8.7 5.5 copy-start.6
  8.7 5.5 copy-start.5
  14.3 12.2 %copy-start.7 = (s32[256,4]{0,1:T(4,128)S(1)}, s32[256,4]{0,1:T(4,128)}, u32[]{:S(2)}) copy-start(s32[256,4]{0,1:T(4,128)} %param.18) | copy-start | bytes 12292
  18.5 33.1 %all-to-all-start.1 = ((f32[32,16,1024]{2,1,0:T(8,128)}), f32[32,16,1024]{2,1,0:T(8,128)}, u32[]{:S(2)}, u32[]{:S(2)}) async-start(f32[32,16,1024]{2,1,0:T(8,128)} %fusion.23), calls=%async_computation.1 | async-start | bytes 4194304 | tf_op jit(solution)/shard_map/all_to_all | solution.py:20
  54.5 51.7 %all-to-all-start.2 = ((bf16[32,16,1024]{2,1,0:T(8,128)(2,1)}), bf16[32,16,1024]{2,1,0:T(8,128)(2,1)}, u32[]{:S(2)}, u32[]{:S(2)}) async-start(bf16[32,16,1024]{2,1,0:T(8,128)(2,1)} %broadcast_in_dim.8), calls=%async_computation.2 | async-start | bytes 2097152 | tf_op jit(solution)/shard_map/all_to_all | solution.py:32
  106.3 16.7 %copy-start.8 = (s32[8,3]{0,1:T(4,128)S(1)}, s32[8,3]{0,1:T(4,128)}, u32[]{:S(2)}) copy-start(s32[8,3]{0,1:T(4,128)} %param.17) | copy-start | bytes 292
  106.3 291.7 %all-to-all-start = ((bf16[32,2,128,2,512]{4,3,2,1,0:T(2,128)(2,1)}), bf16[32,2,128,2,512]{4,3,2,1,0:T(2,128)(2,1)}, u32[]{:S(2)}, u32[]{:S(2)}) async-start(bf16[32,2,128,2,512]{4,3,2,1,0:T(2,128)(2,1)} %copy.61), calls=%async_computation | async-start | bytes 33554432 | tf_op jit(solution)/shard_map/all_to_all | solution.py:125
  116.8 252.3 %collective-permute-start = (bf16[256,2,512]{2,0,1:T(8,128)(2,1)}, bf16[256,2,512]{2,0,1:T(8,128)(2,1)}, u32[]{:S(2)}, u32[]{:S(2)}) collective-permute-start(bf16[256,2,512]{2,0,1:T(8,128)(2,1)} %get-tuple-element.111), channel_id=1, source_target_pairs={{0,4},{4,8},{8,12},{12,16},{16,20},{20,24},{24,28},{28,32},{32,36}... | collective-permute-start | bytes 1572872 | tf_op jit(solution)/shard_map/ppermute | solution.py:46
  120.2 269.3 %collective-permute-start.1 = (bf16[256,2,512]{2,0,1:T(8,128)(2,1)}, bf16[256,2,512]{2,0,1:T(8,128)(2,1)}, u32[]{:S(2)}, u32[]{:S(2)}) collective-permute-start(bf16[256,2,512]{2,0,1:T(8,128)(2,1)} %get-tuple-element.112), channel_id=1, source_target_pairs={{4,0},{8,4},{12,8},{16,12},{20,16},{24,20},{28,24},{32,28},{36,32}... | collective-permute-start | bytes 1572872 | tf_op jit(solution)/shard_map/ppermute | solution.py:49
  123.1 8.3 %copy-start.9 = (s32[8,2]{0,1:T(2,128)S(1)}, s32[8,2]{0,1:T(2,128)}, u32[]{:S(2)}) copy-start(s32[8,2]{0,1:T(2,128)} %param.19) | copy-start | bytes 196
  438.9 2.8 copy-start.2
  462.0 8.8 %copy-start.4 = (bf16[2,4,128,4,128]{4,3,2,1,0:T(4,128)(2,1)S(1)}, bf16[2,4,128,4,128]{4,3,2,1,0:T(4,128)(2,1)}, u32[]{:S(2)}) copy-start(bf16[2,4,128,4,128]{4,3,2,1,0:T(4,128)(2,1)} %get-tuple-element.206) | copy-start | bytes 3145732 | tf_op jit(solution)/shard_map/while
  472.7 3.6 copy-start.1
  537.6 2.8 copy-start.2
  560.7 8.8 %copy-start.4 = (bf16[2,4,128,4,128]{4,3,2,1,0:T(4,128)(2,1)S(1)}, bf16[2,4,128,4,128]{4,3,2,1,0:T(4,128)(2,1)}, u32[]{:S(2)}) copy-start(bf16[2,4,128,4,128]{4,3,2,1,0:T(4,128)(2,1)} %get-tuple-element.206) | copy-start | bytes 3145732 | tf_op jit(solution)/shard_map/while
  571.4 3.6 copy-start.1
where the time goes:
time: 660 us; the launch traced here: 657 us
  waiting for transfers between devices  283 us (43%)
  local copies, waits for them, and re-layouts  217 us (33%)
  blocking collectives  53.7 us (8%)
  matrix products  40.9 us (6%)
  other arithmetic  31.5 us (5%)
  starting transfers between devices  30.6 us (5%)
    ppermute x1, waiting for transfers between devices, with_halo(): lax.ppermute(lax.slice_in_dim(block, block.shape[dim] - width, None, axis...  238 us
    all_to_all x1, blocking collectives, sent_and_summed(): lax.all_to_all(parts, axis, split_axis=0, concat_axis=0, tiled=True)  53.7 us
    gather x4, local copies, waits for them, and re-layouts, attend(): fetched[random_ids]  41.6 us
    gather x2, local copies, waits for them, and re-layouts, per_device(): outgoing = blocks[send_index]  39.7 us
    reshape x2, local copies, waits for them, and re-layouts, attend(): gathered = gathered.reshape(group_size, key_count, 2, head_count, HD)  27.9 us
    gather x4, local copies, waits for them, and re-layouts, attend(): nearby[window_ids]  27.8 us
    all_to_all x1, waiting for transfers between devices, summed_on_arrival(): parts = lax.all_to_all(cut_along(array, dim, count), axis, 0, 0, tiled=True)  24.8 us
    while x14, local copies, waits for them, and re-layouts  21.1 us
  transfers between devices with their start and end apart: 5, of which 3 were waited for; matrix products, arithmetic and copies ran while one was open for 10% of the time, Pallas kernels for 0%

commit v1 on v0

v1 whole, which is shorter than its diff:
```python
import functools

import jax
import jax.numpy as jnp
from jax import lax
from jax.experimental import pallas as pl
from jax.experimental.pallas import tpu as pltpu
from jax.sharding import PartitionSpec as P

HD = 128
BLK = 128
ROWS = 1024
SUMS = 16
SLAB = ROWS + SUMS
LISTS = 9
MESH = pl.DeviceIdType.MESH
ORDER = (0, 1, 3, 2)
ANY = pl.BlockSpec(memory_space=pl.ANY)
VMEM = pl.BlockSpec(memory_space=pltpu.VMEM)
SMEM = pl.BlockSpec(memory_space=pltpu.SMEM)


def place():
    seq = lax.axis_index("seq")
    head = lax.axis_index("head")
    return seq // 16, (seq // 4) % 4, seq % 4, head // 2, head % 2


def device(xl, y, z, xh, c):
    return (xl * 16 + y * 4 + z, xh * 2 + c)


def project_kernel(
    tok_hbm, wk_hbm, wv_hbm, wq_hbm, first_ref, last_ref, kv_ref, q_ref, tok, w, tok_sem, w_sem
):
    parts = 4
    step = ROWS // parts
    weights = (wk_hbm, wv_hbm, wq_hbm)
    tok_copies = [
        pltpu.make_async_copy(
            tok_hbm.at[pl.ds(r * step, step)], tok.at[pl.ds(r * step, step)], tok_sem.at[r]
        )
        for r in range(parts)
    ]
    w_copies = [pltpu.make_async_copy(weights[t], w.at[t], w_sem.at[t]) for t in range(3)]
    w_copies[0].start()
    for copy in tok_copies:
        copy.start()
    w_copies[1].start()
    w_copies[2].start()
    position = lax.broadcasted_iota(jnp.int32, (SUMS, ROWS), 1)
    first = first_ref[...]
    last = last_ref[...]
    member = ((position >= first) & (position < last)).astype(jnp.float32).astype(jnp.bfloat16)
    counts = (last - first).astype(jnp.float32)
    for t in range(3):
        w_copies[t].wait()
        for r in range(parts):
            if t == 0:
                tok_copies[r].wait()
            rows = pl.ds(r * step, step)
            out = jnp.dot(tok[rows], w[t], preferred_element_type=jnp.float32).astype(jnp.bfloat16)
            for j in range(4):
                piece = out[:, j * HD : (j + 1) * HD]
                if t < 2:
                    kv_ref[j, t, rows] = piece
                else:
                    q_ref[j, rows] = piece
        if t < 2:
            for j in range(4):
                sums = jnp.dot(
                    member, kv_ref[j, t, pl.ds(0, ROWS)], preferred_element_type=jnp.float32
                )
                kv_ref[j, t, pl.ds(ROWS, SUMS)] = (sums / counts).astype(jnp.bfloat16)


def project(tokens, w_key, w_value, w_query, first, last):
    return pl.pallas_call(
        project_kernel,
        out_shape=(
            jax.ShapeDtypeStruct((4, 2, SLAB, HD), jnp.bfloat16),
            jax.ShapeDtypeStruct((4, ROWS, HD), jnp.bfloat16),
        ),
        in_specs=[ANY] * 4 + [VMEM] * 2,
        out_specs=(VMEM, VMEM),
        scratch_shapes=[
            pltpu.VMEM(tokens.shape, jnp.bfloat16),
            pltpu.VMEM((3, *w_key.shape), jnp.bfloat16),
            pltpu.SemaphoreType.DMA((4,)),
            pltpu.SemaphoreType.DMA((3,)),
        ],
        name="project",
    )(tokens, w_key, w_value, w_query, first, last)


def spread_kernel(
    kv_ref, q_ref, list_ref, wo_ref,
    kvall_ref, qall_ref, lists_ref, wcols_ref,
    stage,
    in_send, in_recv, q_send, q_recv, l_send, l_recv, w_send, w_recv,
    up_send, up_recv, down_send, down_recv, upk_send, upk_recv, downv_send, downv_recv,
    core_send, core_recv, local_sem,
):
    xl, y, z, xh, c = place()
    seq = lax.axis_index("seq")
    head = lax.axis_index("head")
    above, below = (z + 1) % 4, (z + 3) % 4
    across = (z + 2) % 4
    mine = xl == c
    up_dev = device(xl, y, above, xh, c)
    down_dev = device(xl, y, below, xh, c)
    twin = device(xl, y, z, xh, 1 - c)

    def partner(d):
        return device(c, (y + d) % 4, z, xh, xl)

    barrier = pltpu.get_barrier_semaphore()

    def greet(target):
        pl.semaphore_signal(barrier, inc=1, device_id=target, device_id_type=MESH)

    for d in (1, 2, 3):
        greet(partner(d))
        greet((seq, (head + d) % 4))
    greet(up_dev)
    greet(down_dev)

    @pl.when(jnp.logical_not(mine))
    def _():
        greet(partner(0))

    pl.semaphore_wait(barrier, 8 + (xl + c) % 2)

    def remote(src, dst, send, recv, target):
        return pltpu.make_async_remote_copy(
            src_ref=src, dst_ref=dst, send_sem=send, recv_sem=recv,
            device_id=target, device_id_type=MESH,
        )

    def kv_in(d):
        j = (y + d) % 4
        return remote(kv_ref.at[j], kvall_ref.at[seq], in_send.at[d], in_recv.at[y], partner(d))

    def q_in(d):
        j = (y + d) % 4
        return remote(q_ref.at[j], qall_ref.at[y], q_send.at[d], q_recv.at[y], partner(d))

    def l_in(d):
        return remote(list_ref, lists_ref.at[y], l_send.at[d], l_recv.at[y], partner(d))

    def w_in(k):
        target = (head + k) % 4
        columns = pl.ds(pl.multiple_of(target * 512, 512), 512)
        return remote(
            wo_ref.at[:, columns], wcols_ref.at[head], w_send.at[k - 1], w_recv.at[k - 1],
            (seq, target),
        )

    stage_in = pltpu.make_async_copy(kv_ref.at[y], stage, local_sem.at[0])
    stage_out = pltpu.make_async_copy(stage, kvall_ref.at[seq], local_sem.at[0])
    q_local = pltpu.make_async_copy(q_ref.at[y], qall_ref.at[y], local_sem.at[1])
    l_local = pltpu.make_async_copy(list_ref, lists_ref.at[y], local_sem.at[2])
    w_local = pltpu.make_async_copy(
        wo_ref.at[:, pl.ds(pl.multiple_of(head * 512, 512), 512)], wcols_ref.at[head],
        local_sem.at[3],
    )

    @pl.when(mine)
    def _():
        stage_in.start()

    @pl.when(jnp.logical_not(mine))
    def _():
        kv_in(0).start()

    for d in ORDER[1:]:
        kv_in(d).start()

    @pl.when(mine)
    def _():
        stage_in.wait()
        stage_out.start()

    @pl.when(jnp.logical_not(mine))
    def _():
        q_in(0).start()
        l_in(0).start()

    for d in ORDER[1:]:
        q_in(d).start()
        l_in(d).start()
    w_local.start()
    for k in (2, 1, 3):
        w_in(k).start()

    def row(yy, zz):
        return c * 16 + yy * 4 + zz

    def up_own(yy, s):
        return remote(kvall_ref.at[s], kvall_ref.at[s], up_send.at[yy], up_recv.at[yy], up_dev)

    def down_own(yy, s):
        return remote(
            kvall_ref.at[s], kvall_ref.at[s], down_send.at[yy], down_recv.at[yy], down_dev
        )

    def up_relay(yy, s):
        return remote(
            kvall_ref.at[s, 0], kvall_ref.at[s, 0], upk_send.at[yy], upk_recv.at[yy], up_dev
        )

    def down_relay(yy, s):
        return remote(
            kvall_ref.at[s, 1], kvall_ref.at[s, 1], downv_send.at[yy], downv_recv.at[yy], down_dev
        )

    def to_twin(yy, k, s):
        return remote(
            kvall_ref.at[s], kvall_ref.at[s], core_send.at[yy, k], core_recv.at[yy, k], twin
        )

    for step in range(6):
        if step < 4:
            d = ORDER[step]
            yy = (y + d) % 4
            s = row(yy, z)
            arrived = remote(
                kv_ref.at[0], kvall_ref.at[s], in_send.at[d], in_recv.at[yy], partner(d)
            )
            if d == 0:

                @pl.when(mine)
                def _():
                    stage_out.wait()

                @pl.when(jnp.logical_not(mine))
                def _():
                    arrived.wait_recv()

            else:
                arrived.wait_recv()
            up_own(yy, s).start()
            down_own(yy, s).start()
            to_twin(yy, 0, s).start()
        if 1 <= step < 5:
            yy = (y + ORDER[step - 1]) % 4
            s = row(yy, below)
            up_own(yy, s).wait_recv()
            up_relay(yy, s).start()
            to_twin(yy, 1, s).start()
            s = row(yy, above)
            down_own(yy, s).wait_recv()
            down_relay(yy, s).start()
            to_twin(yy, 2, s).start()
        if 2 <= step:
            yy = (y + ORDER[step - 2]) % 4
            s = row(yy, across)
            up_relay(yy, s).wait_recv()
            down_relay(yy, s).wait_recv()
            to_twin(yy, 3, s).start()

    for d in ORDER:
        j = (y + d) % 4

        def finish():
            kv_in(d).wait_send()
            q_in(d).wait_send()
            l_in(d).wait_send()
            remote(
                q_ref.at[0], qall_ref.at[j], q_send.at[d], q_recv.at[j], partner(d)
            ).wait_recv()
            remote(
                list_ref, lists_ref.at[j], l_send.at[d], l_recv.at[j], partner(d)
            ).wait_recv()

        if d == 0:

            @pl.when(jnp.logical_not(mine))
            def _():
                finish()

            @pl.when(mine)
            def _():
                q_local.start()
                l_local.start()
                q_local.wait()
                l_local.wait()

        else:
            finish()
    w_local.wait()
    for k in (1, 2, 3):
        w_in(k).wait_send()
        source = (head + 4 - k) % 4
        remote(
            wo_ref.at[:, pl.ds(0, 512)], wcols_ref.at[source], w_send.at[k - 1],
            w_recv.at[k - 1], (seq, source),
        ).wait_recv()
    for i in range(4):
        yy = (y + ORDER[i]) % 4
        up_own(yy, row(yy, z)).wait_send()
        down_own(yy, row(yy, z)).wait_send()
        up_relay(yy, row(yy, below)).wait_send()
        down_relay(yy, row(yy, above)).wait_send()
        for k, zz in enumerate((z, below, above, across)):
            to_twin(yy, k, row(yy, zz)).wait_send()
            to_twin(yy, k, (1 - c) * 16 + yy * 4 + zz).wait_recv()


def spread(kv, q, lists, w_out):
    four = pltpu.SemaphoreType.DMA((4,))
    grid4 = pltpu.SemaphoreType.DMA((4, 4))
    return pl.pallas_call(
        spread_kernel,
        out_shape=(
            jax.ShapeDtypeStruct((32, 2, SLAB, HD), jnp.bfloat16),
            jax.ShapeDtypeStruct((4, ROWS, HD), jnp.bfloat16),
            jax.ShapeDtypeStruct((4, 8, 128), jnp.int32),
            jax.ShapeDtypeStruct((4, 512, 512), jnp.bfloat16),
        ),
        in_specs=[ANY] * 4,
        out_specs=(ANY,) * 4,
        scratch_shapes=[pltpu.VMEM((2, SLAB, HD), jnp.bfloat16)]
        + [four] * 16
        + [grid4, grid4, four],
        compiler_params=pltpu.CompilerParams(collective_id=0, has_side_effects=True),
        name="spread",
    )(kv, q, lists, w_out)


def attend_kernel(lists_ref, kv_ref, q_ref, o_ref, sums):
    for t in range(32):
        home = (t + 16) % 32
        for k in range(2):
            sums[k, t // 8, pl.ds((t % 8) * SUMS, SUMS)] = kv_ref[home, k, pl.ds(ROWS, SUMS)]
    factor = HD ** (-0.5) * 1.4426950408889634

    def block(i, carry):
        run = i // 8
        within = i % 8
        rows = pl.ds(pl.multiple_of(within * BLK, BLK), BLK)
        query = q_ref[run, rows]
        keys, vals = [], []
        for n in range(LISTS):
            b = lists_ref[run, within, n]
            if n < LISTS - 2:
                span = pl.ds(pl.multiple_of((b % 8) * BLK, BLK), BLK)
                keys.append(kv_ref[b // 8, 0, span])
                vals.append(kv_ref[b // 8, 1, span])
            else:
                keys.append(sums[0, b])
                vals.append(sums[1, b])
        key = jnp.concatenate(keys, axis=0)
        val = jnp.concatenate(vals, axis=0)
        scores = lax.dot_general(
            query, key, (((1,), (1,)), ((), ())), preferred_element_type=jnp.float32
        )
        peak = jnp.max(scores, axis=1, keepdims=True)
        weights = jnp.exp2((scores - peak) * factor)
        total = jnp.sum(weights, axis=1, keepdims=True)
        out = jnp.dot(weights.astype(jnp.bfloat16), val, preferred_element_type=jnp.float32)
        o_ref[run, rows] = (out / total).astype(jnp.bfloat16)
        return carry

    lax.fori_loop(0, 32, block, 0, unroll=2)


def attend(lists, kv, q):
    return pl.pallas_call(
        attend_kernel,
        out_shape=jax.ShapeDtypeStruct((4, ROWS, HD), jnp.bfloat16),
        in_specs=[SMEM, VMEM, VMEM],
        out_specs=VMEM,
        scratch_shapes=[pltpu.VMEM((2, 4, BLK, HD), jnp.bfloat16)],
        name="attend",
    )(lists, kv, q)


def collect_kernel(o_ref, all_ref, send, recv, core_send, core_recv, local_sem):
    xl, y, z, xh, c = place()
    mine = xl == c
    twin = device(xl, y, z, xh, 1 - c)

    def partner(d, e):
        return device(c, (y + d) % 4, z, (xh + e) % 2, xl)

    barrier = pltpu.get_barrier_semaphore()

    def greet(target):
        pl.semaphore_signal(barrier, inc=1, device_id=target, device_id_type=MESH)

    greet(twin)
    for d in range(4):
        greet(partner(d, 1))
        if d > 0:
            greet(partner(d, 0))

    @pl.when(jnp.logical_not(mine))
    def _():
        greet(partner(0, 0))

    pl.semaphore_wait(barrier, 8 + (xl + c) % 2)

    def remote(src, dst, send, recv, target):
        return pltpu.make_async_remote_copy(
            src_ref=src, dst_ref=dst, send_sem=send, recv_sem=recv,
            device_id=target, device_id_type=MESH,
        )

    my_head = (xh * 2 + xl) * 4 + y

    def out(d, e):
        return remote(
            o_ref.at[(y + d) % 4], all_ref.at[my_head], send.at[d, e], recv.at[y, e],
            partner(d, e),
        )

    local = pltpu.make_async_copy(o_ref.at[y], all_ref.at[my_head], local_sem)

    @pl.when(mine)
    def _():
        local.start()

    for d in (2, 1, 3, 0):
        out(d, 1).start()
        if d > 0:
            out(d, 0).start()
        else:

            @pl.when(jnp.logical_not(mine))
            def _():
                out(0, 0).start()

    def to_twin(yy, e, h):
        return remote(
            all_ref.at[h], all_ref.at[h], core_send.at[yy, e], core_recv.at[yy, e], twin
        )

    for d in ORDER:
        yy = (y + d) % 4
        for e in (0, 1):
            h = (((xh + e) % 2) * 2 + c) * 4 + yy
            arrived = remote(
                o_ref.at[0], all_ref.at[h], send.at[d, e], recv.at[yy, e], partner(d, e)
            )
            if d == 0 and e == 0:

                @pl.when(mine)
                def _():
                    local.wait()

                @pl.when(jnp.logical_not(mine))
                def _():
                    arrived.wait_recv()

            else:
                arrived.wait_recv()
            to_twin(yy, e, h).start()
    for d in ORDER:
        yy = (y + d) % 4
        for e in (0, 1):
            if d == 0 and e == 0:

                @pl.when(jnp.logical_not(mine))
                def _():
                    out(0, 0).wait_send()

            else:
                out(d, e).wait_send()
            h = (((xh + e) % 2) * 2 + c) * 4 + yy
            to_twin(yy, e, h).wait_send()
            other = (((xh + e) % 2) * 2 + 1 - c) * 4 + yy
            to_twin(yy, e, other).wait_recv()


def collect(attended):
    return pl.pallas_call(
        collect_kernel,
        out_shape=jax.ShapeDtypeStruct((16, ROWS, HD), jnp.bfloat16),
        in_specs=[ANY],
        out_specs=ANY,
        scratch_shapes=[
            pltpu.SemaphoreType.DMA((4, 2)),
            pltpu.SemaphoreType.DMA((4, 2)),
            pltpu.SemaphoreType.DMA((4, 2)),
            pltpu.SemaphoreType.DMA((4, 2)),
            pltpu.SemaphoreType.DMA,
        ],
        compiler_params=pltpu.CompilerParams(collective_id=1, has_side_effects=True),
        name="collect",
    )(attended)


def mix_kernel(a_ref, w_ref, o_ref):
    rows = jnp.concatenate([a_ref[h] for h in range(16)], axis=1)
    o_ref[...] = jnp.dot(rows, w_ref[...], preferred_element_type=jnp.float32).astype(jnp.bfloat16)


def mix(attended, w_cols):
    step = 256
    return pl.pallas_call(
        mix_kernel,
        grid=(ROWS // step,),
        out_shape=jax.ShapeDtypeStruct((ROWS, 512), jnp.bfloat16),
        in_specs=[
            pl.BlockSpec((16, step, HD), lambda i: (0, i, 0)),
            pl.BlockSpec((2048, 512), lambda i: (0, 0), pipeline_mode=pl.Buffered(1)),
        ],
        out_specs=pl.BlockSpec((step, 512), lambda i: (i, 0)),
        name="mix",
    )(attended, w_cols)


def per_device(
    tokens, w_query, w_key, w_value, w_out,
    window_blocks, random_blocks, summary_blocks, seg_start, seg_end,
):
    seq = lax.axis_index("seq")
    own = ((seq + 16) % 32) * SUMS
    first = lax.dynamic_slice_in_dim(seg_start, own, SUMS)[:, None] - seq * ROWS
    last = lax.dynamic_slice_in_dim(seg_end, own, SUMS)[:, None] - seq * ROWS
    random_own = lax.dynamic_slice_in_dim(random_blocks, seq * 8, 8)
    lists = jnp.concatenate([window_blocks, random_own, summary_blocks], axis=1)
    lists = jnp.pad(lists, ((0, 0), (0, 128 - LISTS)))
    kv, q = project(tokens, w_key, w_value, w_query, first, last)
    kvall, qall, lists_all, w_cols = spread(kv, q, lists, w_out)
    attended = attend(lists_all, kvall, qall)
    everything = collect(attended)
    return mix(everything, w_cols.reshape(2048, 512))


def solution(mesh):
    placed = (
        P("seq", None),
        P(None, "head"),
        P(None, "head"),
        P(None, "head"),
        P("head", None),
        P("seq", None),
        P(),
        P("seq", None),
        P(),
        P(),
    )
    return jax.shard_map(
        per_device, mesh=mesh, in_specs=placed, out_specs=P("seq", "head"), check_vma=False
    )
```

time: 660 us -> 168 us (0.25)
  the two profiles are of different devices: /device:TPU:120 before, /device:TPU:1 now
where the time goes in v1:
time: 168 us
  Pallas kernels  163 us (97%)
  local copies, waits for them, and re-layouts  3.62 us (2%)
    pallas_call x1, Pallas kernels, spread(): pl.pallas_call(spread_kernel, out_shape=(jax.ShapeDtypeStruct((32, 2, SLA...  84.6 us
    pallas_call x1, Pallas kernels, collect(): pl.pallas_call(collect_kernel, out_shape=jax.ShapeDtypeStruct((16, ROWS,...  38.1 us
    pallas_call x1, Pallas kernels, attend(): pl.pallas_call(attend_kernel, out_shape=jax.ShapeDtypeStruct((4, ROWS, HD...  22.8 us
    pallas_call x1, Pallas kernels, project(): pl.pallas_call(project_kernel, out_shape=(jax.ShapeDtypeStruct((4, 2, SLA...  11.6 us
    pallas_call x1, Pallas kernels, mix(): pl.pallas_call(mix_kernel, grid=(ROWS // step,), out_shape=jax.ShapeDtype...  6.2 us

profile of v1, /device:TPU:1, one launch (start us, length us, event | category | flops | bytes accessed | tf_op | source)
XLA Modules:
  0.0 167.8 jit_solution(17216054944961493747)
XLA Ops:
  0.0 0.0 copy-start
  0.0 0.8 subtract_bitcast_fusion
  0.8 0.0 copy-done
  0.8 0.1 constant_dynamic-slice_fusion
  0.9 0.1 copy.16
  0.9 0.8 copy.14
  1.7 0.8 copy.15
  2.5 0.1 pad_add_fusion
  2.5 0.6 pad.4.list_ref
  3.1 0.7 copy.12.last_ref
  3.8 0.7 copy.11.first_ref
  4.5 11.6 %project.1 = (bf16[4,2,1040,128]{3,2,1,0:T(8,128)(2,1)}, bf16[4,1024,128]{2,1,0:T(8,128)(2,1)}) custom-call(bf16[1024,2048]{1,0:T(8,128)(2,1)} %tok_hbm.1, bf16[2048,512]{1,0:T(8,128)(2,1)} %wk_hbm.1, bf16[2048,512]{1,0:T(8,128)(2,1)} %wv_hbm.1, bf16[2048,512]{1,0:T(8,128)(2,1)} %wq_hbm.1, s32[16,1]{1,0:T(8,128)} %copy.11.first_ref, s32[16,1]{1,0:T(8,128)} %copy.12.last_ref), custom_call_target="tpu_custom_call" | custom-call | tf_op jit(solution)/shard_map/project/pallas_call | solution.py:78
  16.1 84.6 %spread.1 = (bf16[32,2,1040,128]{3,2,1,0:T(8,128)(2,1)}, bf16[4,1024,128]{2,1,0:T(8,128)(2,1)}, s32[4,8,128]{2,1,0:T(8,128)}, bf16[4,512,512]{2,1,0:T(8,128)(2,1)}) custom-call(bf16[4,2,1040,128]{3,2,1,0:T(8,128)(2,1)} %get-tuple-element.11.kv_ref, bf16[4,1024,128]{2,1,0:T(8,128)(2,1)} %get-tuple-element.12.q_ref, s32[8,128]{1,0:T(8,128)} %pad.4.list_ref, ...), custom_call_target="tpu_custom_call" | custom-call | tf_op jit(solution)/shard_map/spread/pallas_call | solution.py:313
  100.7 22.8 %attend.1.o_ref = bf16[4,1024,128]{2,1,0:T(8,128)(2,1)} custom-call(s32[4,8,128]{2,1,0:T(8,128)} %get-tuple-element.13.lists_ref, bf16[32,2,1040,128]{3,2,1,0:T(8,128)(2,1)} %get-tuple-element.14.kv_ref, bf16[4,1024,128]{2,1,0:T(8,128)(2,1)} %get-tuple-element.15.q_ref), custom_call_target="tpu_custom_call" | custom-call | tf_op jit(solution)/shard_map/attend/pallas_call | solution.py:369
  123.6 38.1 %collect.1.a_ref = bf16[16,1024,128]{2,1,0:T(8,128)(2,1)} custom-call(bf16[4,1024,128]{2,1,0:T(8,128)(2,1)} %attend.1.o_ref), custom_call_target="tpu_custom_call" | custom-call | tf_op jit(solution)/shard_map/collect/pallas_call | solution.py:477
  161.6 6.2 %mix.1 = bf16[1024,512]{1,0:T(8,128)(2,1)} custom-call(bf16[16,1024,128]{2,1,0:T(8,128)(2,1)} %collect.1.a_ref, bf16[2048,512]{1,0:T(8,128)(2,1)} %bitcast.5), custom_call_target="tpu_custom_call" | custom-call | tf_op jit(solution)/shard_map/mix/pallas_call | solution.py:501
Async XLA Ops:
  0.0 0.8 copy-start
